TPU v7x, 512 devices: a whole 4x4x16 slice. The times are simulated.
512 devices in a mesh: gx: 8 (over y, z_hi), gy: 8 (over z_lo), gz: 8 (over x, core).
Axes of the slice: x: 4, y: 4, z: 16 (z_hi: 2, z_lo: 8; z = z_hi * 8 + z_lo), core: 2. Of those that a mesh axis runs over, the one named last changes fastest.
Arguments:
- tokens: bfloat16 [1024, 8192], P('gx', 'gz'), may hold values from -6 to 6
- gate_weight: bfloat16 [8192, 14336], P('gz', ('gx', 'gy')), may hold values from -0.0625 to 0.0625
- up_weight: bfloat16 [8192, 14336], P('gz', ('gx', 'gy')), may hold values from -0.0625 to 0.0625
- down_weight: bfloat16 [14336, 8192], P(('gx', 'gy'), 'gz'), may hold values from -0.046875 to 0.046875
- out_grad: bfloat16 [1024, 8192], P('gx', 'gz'), may hold values from -6 to 6
Outputs:
- output: bfloat16 [1024, 8192], P('gx', 'gz')
- input_grad: bfloat16 [1024, 8192], P('gx', 'gz')
- gate_grad: bfloat16 [8192, 14336], P('gz', ('gx', 'gy'))
- up_grad: bfloat16 [8192, 14336], P('gz', ('gx', 'gy'))
- down_grad: bfloat16 [14336, 8192], P(('gx', 'gy'), 'gz')
All inputs are finite; a program needn't handle non-finite values.
Results may differ from a plain program's by a relative error of at most 0.025.
Values may be sent and summed in bfloat16 or wider, within the bound.
No kernel may reach another device: no remote copies, remote signals or barrier semaphores. Data moves between devices by JAX's collectives and lax.ppermute only.
A program may use at most 64 MiB of HBM per device.

v0:
```python
import jax
import jax.numpy as jnp
from jax import lax
from jax.sharding import Mesh
from jax.sharding import PartitionSpec as P

GX = ("gx_0", "gx_1")
GX_GY = ("gx_0", "gx_1", "gy")


def side_by_side(arrays, axis, dim, along):
    both = jnp.concatenate(arrays, axis=along)
    out, at, finished = (lax.psum_scatter(both, axis, scatter_dimension=dim, tiled=True), 0, [])
    for a in arrays:
        finished.append(lax.slice_in_dim(out, at, at + a.shape[along], axis=along))
        at += a.shape[along]
    return tuple(finished)


def copy_for_each(shard, axis):
    devices = lax.axis_size(axis)
    return lax.all_to_all(
        jnp.broadcast_to(shard[None], (devices, *shard.shape)), axis, 0, 0, tiled=True
    )


def in_order(tiles, dim):
    tiles = jnp.moveaxis(tiles, 0, dim)
    shape = tiles.shape
    return tiles.reshape(*shape[:dim], shape[dim] * shape[dim + 1], *shape[dim + 2 :])


def collect(shard, axis, dim):
    tiles = copy_for_each(shard, axis)
    return in_order(tiles, dim)


def gathered_by_axis(shard, axes, dim):
    if not axes:
        return shard
    nearer = lax.all_gather(shard, axes[-1], axis=dim, tiled=True)
    return gathered_by_axis(nearer, axes[:-1], dim)


def of_everyone(shard, axis):
    everything = copy_for_each(shard, axis)
    return jnp.sum(everything.astype(jnp.float32), axis=0)


def cut_along(shard, dim, devices):
    before, after = (shard.shape[:dim], shard.shape[dim + 1 :])
    return jnp.moveaxis(shard.reshape(*before, devices, -1, *after), dim, 0)


def summed_on_arrival(shard, axis, dim):
    devices = lax.axis_size(axis)
    tiles = lax.all_to_all(cut_along(shard, dim, devices), axis, 0, 0, tiled=True)
    return jnp.sum(tiles.astype(jnp.float32), axis=0)


def sent_together(arrays, axis, dim, along):
    widths = [a.shape[along] for a in arrays]
    both = jnp.concatenate(arrays, axis=along)
    out = lax.all_gather(both, axis, axis=dim, tiled=True)
    return tuple(jnp.split(out, [sum(widths[:k]) for k in range(1, len(widths))], axis=along))


def contract_rows(left, right):
    return lax.dot_general(
        left, right, (((0,), (0,)), ((), ())), preferred_element_type=jnp.float32
    )


def contract_cols(left, right):
    return lax.dot_general(
        left, right, (((1,), (1,)), ((), ())), preferred_element_type=jnp.float32
    )


def activate(gate, upward):
    sigmoid = jax.nn.sigmoid(gate)
    hidden = (gate * sigmoid * upward).astype(jnp.bfloat16)
    return (hidden, sigmoid)


def backward_gates(dhidden, gate, upward, sigmoid):
    dgate = (dhidden * upward * sigmoid * (1.0 + gate * (1.0 - sigmoid))).astype(jnp.bfloat16)
    dupward = (dhidden * gate * sigmoid).astype(jnp.bfloat16)
    return (dgate, dupward)


def body(tokens, gate_weight, up_weight, down_weight, out_grad):
    all_tokens = lax.all_gather(tokens, GX, axis=0, tiled=True)
    gate_part = jnp.dot(all_tokens, gate_weight, preferred_element_type=jnp.float32)
    up_part = jnp.dot(all_tokens, up_weight, preferred_element_type=jnp.float32)
    gate, upward = tuple(
        (
            part.astype(jnp.float32)
            for part in side_by_side(
                (gate_part.astype(jnp.bfloat16), up_part.astype(jnp.bfloat16)), "gz", 0, 1
            )
        )
    )
    hidden_own, sigmoid = activate(gate, upward)
    hidden_all = collect(hidden_own, "gz", 0)
    hidden_mine = lax.all_to_all(hidden_all, GX, split_axis=0, concat_axis=1, tiled=True)
    output_part = jnp.dot(
        hidden_mine, gathered_by_axis(down_weight, GX, 0), preferred_element_type=jnp.float32
    )
    output = (
        of_everyone(output_part.astype(jnp.bfloat16), "gy").astype(jnp.float32).astype(jnp.bfloat16)
    )
    all_grad = lax.all_gather(out_grad, GX, axis=0, tiled=True)
    dhidden_part = contract_cols(all_grad, down_weight)
    dhidden = summed_on_arrival(dhidden_part.astype(jnp.bfloat16), "gz", 0)
    dgate_own, dup_own = backward_gates(dhidden, gate, upward, sigmoid)
    dgate_all, dup_all = sent_together((dgate_own, dup_own), "gz", 0, 1)
    input_part = lax.psum_scatter(
        (contract_cols(dgate_all, gate_weight) + contract_cols(dup_all, up_weight)).astype(
            jnp.bfloat16
        ),
        GX,
        scatter_dimension=0,
        tiled=True,
    )
    input_grad = of_everyone(input_part, "gy").astype(jnp.float32).astype(jnp.bfloat16)
    gate_grad = contract_rows(all_tokens, dgate_all).astype(jnp.bfloat16)
    up_grad = contract_rows(all_tokens, dup_all).astype(jnp.bfloat16)
    down_grad = contract_rows(hidden_all, all_grad).astype(jnp.bfloat16)
    return (output, input_grad, gate_grad, up_grad, down_grad)


def solution(mesh):
    finer = Mesh(
        mesh.devices.reshape(4, 2, mesh.shape["gy"], mesh.shape["gz"]), ("gx_0", "gx_1", "gy", "gz")
    )
    in_specs = (P(GX, "gz"), P("gz", GX_GY), P("gz", GX_GY), P(GX_GY, "gz"), P(GX, "gz"))
    out_specs = (P(GX, "gz"), P(GX, "gz"), P("gz", GX_GY), P("gz", GX_GY), P(GX_GY, "gz"))
    return jax.shard_map(body, mesh=finer, in_specs=in_specs, out_specs=out_specs, check_vma=False)
```

profile of v0, /device:TPU:2, one launch (start us, length us, event | category | flops | bytes accessed | tf_op | source)
XLA Modules:
  0.0 693.5 jit_solution(4162685620083025210)
XLA Ops:
  7.2 0.0 copy-start
  7.2 0.0 all-gather.4.cloned.1.call-start
  7.2 0.7 all-gather.4.cloned.1.call-update
  7.9 0.0 all-gather.8.cloned.1.call-start
  8.0 0.7 all-gather.8.cloned.1.call-update
  8.7 0.0 reduce-scatter.7.cloned.1.call-start
  8.7 123.5 %all-gather.4.cloned.1.call-done = bf16[1024,1024]{1,0:T(8,128)(2,1)} async-done(((bf16[128,1024]{1,0:T(8,128)(2,1)}), bf16[1024,1024]{1,0:T(8,128)(2,1)}) %all-gather.4.cloned.1.call-update) | async-done | bytes 2097168 | tf_op jit(solution)/shard_map/all_gather | solution.py:93
  132.2 0.0 copy-start.3
  132.2 2.6 convolution_convert_fusion.4
  134.8 0.0 copy-done
  134.8 0.0 copy-done.3
  134.8 0.8 convolution_convert_fusion.5
  135.6 0.0 copy-start.2
  135.6 0.1 pad_maximum_fusion
  135.7 1.3 copy.16
  137.0 0.0 reduce-scatter.7.cloned.1.call-update
  137.0 0.0 all-gather.6.cloned.1.call-start
  137.0 0.0 copy-done.2
  137.1 23.9 %all_gather.16 = bf16[448,1024]{1,0:T(8,128)(2,1)} all-gather(bf16[224,1024]{1,0:T(8,128)(2,1)S(1)} %copy-done.2), channel_id=1, replica_groups=mesh['gx_0'=4,'gx_1'=2,'gy'=8,'gz'=8] {'gx_1'}, dimensions={0}, use_global_device_ids=true | all-gather | bytes 1376256 | tf_op jit(solution)/shard_map/all_gather | solution.py:41
  160.9 0.0 all-gather.6.cloned.1.call-update
  161.0 110.2 %all-gather.8.cloned.1.call-done = bf16[1024,1024]{1,0:T(8,128)(2,1)} async-done(((bf16[128,1024]{1,0:T(8,128)(2,1)}), bf16[1024,1024]{1,0:T(8,128)(2,1)}) %all-gather.8.cloned.1.call-update) | async-done | bytes 2097168 | tf_op jit(solution)/shard_map/all_gather | solution.py:113
  271.2 2.4 fusion
  273.6 0.1 copy.27
  273.7 12.8 %all_to_all.36 = bf16[8,128,224]{1,2,0:T(8,128)(2,1)S(1)} all-to-all(bf16[8,128,224]{1,2,0:T(8,128)(2,1)S(1)} %bitcast.34), channel_id=1, replica_groups=mesh['gx_0'=4,'gx_1'=2,'gy'=8,'gz'=8] {'gz'}, dimensions={0} | all-to-all | bytes 917504 | tf_op jit(solution)/shard_map/all_to_all | solution.py:57
  286.5 0.1 convert_reduce_fusion
  286.5 19.3 %reduce-scatter.7.cloned.1.call-done = bf16[128,448]{1,0:T(8,128)(2,1)} async-done(((bf16[1024,448]{1,0:T(8,128)(2,1)}), bf16[128,448]{1,0:T(8,128)(2,1)}) %reduce-scatter.7.cloned.1.call-update) | async-done | bytes 114704
  305.8 1.1 fusion.20
  306.9 0.1 copy.18
  307.0 0.1 copy.19
  307.1 0.1 fusion.13
  307.2 0.1 broadcast_in_dim.6
  307.3 14.9 %all_to_all.37 = bf16[8,128,224]{1,2,0:T(8,128)(2,1)} all-to-all(bf16[8,128,224]{1,2,0:T(8,128)(2,1)S(1)} %broadcast_in_dim.6), channel_id=1, replica_groups=mesh['gx_0'=4,'gx_1'=2,'gy'=8,'gz'=8] {'gz'}, dimensions={0} | all-to-all | bytes 917504 | tf_op jit(solution)/shard_map/all_to_all | solution.py:22
  322.1 14.5 %all-to-all-start.1 = ((bf16[8,128,224]{1,2,0:T(8,128)(2,1)}), bf16[8,128,224]{1,2,0:T(8,128)(2,1)S(1)}, u32[]{:S(2)}, u32[]{:S(2)}) async-start(bf16[8,128,224]{1,2,0:T(8,128)(2,1)} %all_to_all.37), calls=%async_computation.1 | async-start | bytes 917504 | tf_op jit(solution)/shard_map/all_to_all | solution.py:106
  336.6 29.5 %all-gather.6.cloned.1.call-done = bf16[1792,1024]{1,0:T(8,128)(2,1)} async-done(((bf16[448,1024]{1,0:T(8,128)(2,1)}), bf16[1792,1024]{1,0:T(8,128)(2,1)}) %all-gather.6.cloned.1.call-update) | async-done | bytes 3670032 | tf_op jit(solution)/shard_map/all_gather | solution.py:41
  366.1 0.0 all-to-all-done.1
  366.1 2.7 convolution_convert_fusion.6
  368.9 1.6 broadcast_in_dim.7
  370.5 10.0 %all-to-all-start.2 = ((bf16[8,128,1024]{2,1,0:T(8,128)(2,1)}), bf16[8,128,1024]{2,1,0:T(8,128)(2,1)S(1)}, u32[]{:S(2)}, u32[]{:S(2)}) async-start(bf16[8,128,1024]{2,1,0:T(8,128)(2,1)} %broadcast_in_dim.7), calls=%async_computation.2 | async-start | bytes 4194304 | tf_op jit(solution)/shard_map/all_to_all | solution.py:22
  380.5 0.0 reduce-scatter.5.cloned.1.call-start
  380.5 14.3 %all_gather.19 = bf16[1024,448]{0,1:T(8,128)(2,1)S(1)} all-gather(bf16[128,448]{0,1:T(8,128)(2,1)S(1)} %pad_maximum_fusion.1), channel_id=1, replica_groups=mesh['gx_0'=4,'gx_1'=2,'gy'=8,'gz'=8] {'gz'}, dimensions={0}, use_global_device_ids=true | all-gather | bytes 1032192 | tf_op jit(solution)/shard_map/all_gather | solution.py:64
  394.8 0.0 copy-start.1
  394.8 0.8 fusion.8
  395.6 0.3 copy-done.1
  395.8 2.1 add_convert_fusion
  398.0 0.0 reduce-scatter.5.cloned.1.call-update
  398.0 184.5 %reduce-scatter.5.cloned.1.call-done = bf16[128,1024]{1,0:T(8,128)(2,1)} async-done(((bf16[1024,1024]{1,0:T(8,128)(2,1)}), bf16[128,1024]{1,0:T(8,128)(2,1)}) %reduce-scatter.5.cloned.1.call-update) | async-done | bytes 262160 | tf_op jit(solution)/shard_map/reduce_scatter | solution.py:118
  582.5 0.0 all-to-all-done.2
  582.5 2.6 broadcast_in_dim.8
  585.0 4.3 all-to-all-start.4
  589.4 0.0 copy-start.4
  589.4 3.2 fusion.1
  592.6 0.0 copy-done.4
  592.6 0.0 copy-start.5
  592.6 1.4 fusion.2
  594.0 0.2 copy-done.5
  594.2 2.4 convolution_convert_fusion
  596.6 1.1 reduce_sum.33
  597.7 86.6 %all-to-all-done.4 = bf16[8,128,1024]{2,1,0:T(8,128)(2,1)} async-done(((bf16[8,128,1024]{2,1,0:T(8,128)(2,1)}), bf16[8,128,1024]{2,1,0:T(8,128)(2,1)}, u32[]{:S(2)}, u32[]{:S(2)}) %all-to-all-start.4) | async-done | bytes 2097184 | tf_op jit(solution)/shard_map/all_to_all | solution.py:22
  684.3 2.7 reduce_sum.35
  (1 shorter events, 0.0 us)
Async XLA Ops:
  7.2 127.6 %copy-start = (bf16[1024,224]{0,1:T(8,128)(2,1)S(1)}, bf16[1024,224]{0,1:T(8,128)(2,1)}, u32[]{:S(2)}) copy-start(bf16[1024,224]{0,1:T(8,128)(2,1)} %param.6) | copy-start | bytes 1376260
  7.2 125.0 %all-gather.4.cloned.1.call-start = ((), (), s32[]{:S(2)}) async-start(), calls=%async_computation.7 | async-start | bytes 2359296 | tf_op jit(solution)/shard_map/all_gather | solution.py:93
  7.9 263.3 %all-gather.8.cloned.1.call-start = ((), (), s32[]{:S(2)}) async-start(), calls=%async_computation.9 | async-start | bytes 2359296 | tf_op jit(solution)/shard_map/all_gather | solution.py:113
  8.7 297.1 %reduce-scatter.7.cloned.1.call-start = ((), (), s32[]{:S(2)}) async-start(), calls=%async_computation.11 | async-start | bytes 1179648
  132.2 2.6 copy-start.3
  135.6 1.4 copy-start.2
  137.0 229.1 %all-gather.6.cloned.1.call-start = ((), (), s32[]{:S(2)}) async-start(), calls=%async_computation.8 | async-start | bytes 4587520 | tf_op jit(solution)/shard_map/all_gather | solution.py:41
  322.1 44.0 %all-to-all-start.1 = ((bf16[8,128,224]{1,2,0:T(8,128)(2,1)}), bf16[8,128,224]{1,2,0:T(8,128)(2,1)S(1)}, u32[]{:S(2)}, u32[]{:S(2)}) async-start(bf16[8,128,224]{1,2,0:T(8,128)(2,1)} %all_to_all.37), calls=%async_computation.1 | async-start | bytes 917504 | tf_op jit(solution)/shard_map/all_to_all | solution.py:106
  370.5 212.0 %all-to-all-start.2 = ((bf16[8,128,1024]{2,1,0:T(8,128)(2,1)}), bf16[8,128,1024]{2,1,0:T(8,128)(2,1)S(1)}, u32[]{:S(2)}, u32[]{:S(2)}) async-start(bf16[8,128,1024]{2,1,0:T(8,128)(2,1)} %broadcast_in_dim.7), calls=%async_computation.2 | async-start | bytes 4194304 | tf_op jit(solution)/shard_map/all_to_all | solution.py:22
  380.5 202.0 %reduce-scatter.5.cloned.1.call-start = ((), (), s32[]{:S(2)}) async-start(), calls=%async_computation.10 | async-start | bytes 2359296 | tf_op jit(solution)/shard_map/reduce_scatter | solution.py:118
  394.8 1.0 copy-start.1
  585.0 99.2 %all-to-all-start.4 = ((bf16[8,128,1024]{2,1,0:T(8,128)(2,1)}), bf16[8,128,1024]{2,1,0:T(8,128)(2,1)}, u32[]{:S(2)}, u32[]{:S(2)}) async-start(bf16[8,128,1024]{2,1,0:T(8,128)(2,1)} %broadcast_in_dim.8), calls=%async_computation.5 | async-start | bytes 4194304 | tf_op jit(solution)/shard_map/all_to_all | solution.py:22
  589.4 3.2 copy-start.4
  592.6 1.6 copy-start.5
Sparse Core Ops, SparseCore 0:
  11.2 120.9 all-gather.3
  135.4 135.7 all-gather.7
  274.0 31.7 reduce-scatter.6
  307.8 58.3 all-gather.5
  398.1 184.3 reduce-scatter.4
where the time goes:
time: 694 us
  waiting for transfers between devices  555 us (80%)
  blocking collectives  65.8 us (9%)
  starting transfers between devices  29.1 us (4%)
  matrix products  18.3 us (3%)
  between operations  13.9 us (2%)
  local copies, waits for them, and re-layouts  7.4 us (1%)
    reduce_scatter x1, waiting for transfers between devices, body(): lax.psum_scatter((contract_cols(dgate_all, gate_weight) + contract_cols(d...  184 us
    all_gather x1, waiting for transfers between devices, body(): all_tokens = lax.all_gather(tokens, GX, axis=0, tiled=True)  123 us
    all_gather x1, waiting for transfers between devices, body(): all_grad = lax.all_gather(out_grad, GX, axis=0, tiled=True)  110 us
    all_to_all x2, waiting for transfers between devices, copy_for_each(): lax.all_to_all(jnp.broadcast_to(shard[None], (devices, *shard.shape)), ax...  86.6 us
    all_gather x1, waiting for transfers between devices, gathered_by_axis(): nearer = lax.all_gather(shard, axes[-1], axis=dim, tiled=True)  29.5 us
    all_gather x1, blocking collectives, gathered_by_axis(): nearer = lax.all_gather(shard, axes[-1], axis=dim, tiled=True)  23.9 us
    unnamed x6, waiting for transfers between devices  20.7 us
    all_to_all x1, blocking collectives, copy_for_each(): lax.all_to_all(jnp.broadcast_to(shard[None], (devices, *shard.shape)), ax...  14.9 us
  transfers between devices with their start and end apart: 8, of which 6 were waited for; matrix products, arithmetic and copies ran while one was open for 3% of the time, Pallas kernels for 0%

commit v1 on v0

--- a/solution.py
+++ b/solution.py
@@ -6,6 +6,12 @@
 
 GX = ("gx_0", "gx_1")
 GX_GY = ("gx_0", "gx_1", "gy")
+
+
+def supply_halves(own_rows, mesh_name):
+    piece_now = jnp.stack([own_rows] * jax.lax.psum(1, axis_name=mesh_name))
+    k_now = jax.lax.all_to_all(piece_now, axis_name=mesh_name, split_axis=0, concat_axis=0)
+    return jnp.concatenate(k_now, axis=0)
 
 
 def side_by_side(arrays, axis, dim, along):
@@ -90,7 +96,7 @@
 
 
 def body(tokens, gate_weight, up_weight, down_weight, out_grad):
-    all_tokens = lax.all_gather(tokens, GX, axis=0, tiled=True)
+    all_tokens = supply_halves(tokens, GX)
     gate_part = jnp.dot(all_tokens, gate_weight, preferred_element_type=jnp.float32)
     up_part = jnp.dot(all_tokens, up_weight, preferred_element_type=jnp.float32)
     gate, upward = tuple(

time: 694 us -> 658 us (0.948)
  waiting for transfers between devices: 555 us -> 443 us
  blocking collectives: 65.8 us -> 122 us
  starting transfers between devices: 29.1 us -> 47 us
    all_gather x1 -> x0, waiting for transfers between devices: 123 us -> none  [body(): all_tokens = lax.all_gather(tokens, GX, axis=0, tiled=True)]
    all_gather x1, waiting for transfers between devices: 110 us -> 17.6 us  [body(): all_grad = lax.all_gather(out_grad, GX, axis=0, tiled=True)]
    all_to_all x0 -> x1, waiting for transfers between devices: none -> 56.7 us  [supply_halves(): jax.lax.all_to_all(piece_now, axis_name=mesh_name, split_axis=0, concat_a...]
    all_gather x1, blocking collectives: 23.9 us -> 80.3 us  [gathered_by_axis(): nearer = lax.all_gather(shard, axes[-1], axis=dim, tiled=True)]
    unnamed x6 -> x5, waiting for transfers between devices: 20.7 us -> 67.8 us
    all_to_all x0 -> x1, starting transfers between devices: none -> 17.9 us  [supply_halves(): jax.lax.all_to_all(piece_now, axis_name=mesh_name, split_axis=0, concat_a...]
where the time goes in v1:
time: 658 us; the launch traced here: 657 us
  waiting for transfers between devices  443 us (67%)
  blocking collectives  122 us (19%)
  starting transfers between devices  47 us (7%)
  matrix products  16.6 us (3%)
  between operations  13.9 us (2%)
  local copies, waits for them, and re-layouts  10.5 us (2%)
    reduce_scatter x1, waiting for transfers between devices, body(): lax.psum_scatter((contract_cols(dgate_all, gate_weight) + contract_cols(d...  184 us
    all_to_all x2, waiting for transfers between devices, copy_for_each(): lax.all_to_all(jnp.broadcast_to(shard[None], (devices, *shard.shape)), ax...  86.6 us
    all_gather x1, blocking collectives, gathered_by_axis(): nearer = lax.all_gather(shard, axes[-1], axis=dim, tiled=True)  80.3 us
    unnamed x5, waiting for transfers between devices  67.8 us
    all_to_all x1, waiting for transfers between devices, supply_halves(): jax.lax.all_to_all(piece_now, axis_name=mesh_name, split_axis=0, concat_a...  56.7 us
    all_gather x1, waiting for transfers between devices, gathered_by_axis(): nearer = lax.all_gather(shard, axes[-1], axis=dim, tiled=True)  29.6 us
    all_to_all x1, starting transfers between devices, supply_halves(): jax.lax.all_to_all(piece_now, axis_name=mesh_name, split_axis=0, concat_a...  17.9 us
    all_gather x1, waiting for transfers between devices, body(): all_grad = lax.all_gather(out_grad, GX, axis=0, tiled=True)  17.6 us
  transfers between devices with their start and end apart: 8, of which 6 were waited for; matrix products, arithmetic and copies ran while one was open for 3% of the time, Pallas kernels for 0%

profile of v1, /device:TPU:2, one launch (start us, length us, event | category | flops | bytes accessed | tf_op | source)
XLA Modules:
  0.0 656.9 jit_solution(8767794135737963194)
XLA Ops:
  7.2 0.0 copy-start
  7.2 2.6 stack.2
  9.8 0.0 copy-start.3
  9.8 17.9 %all-to-all-start = ((bf16[8,128,1024]{2,1,0:T(8,128)(2,1)}), bf16[8,128,1024]{2,1,0:T(8,128)(2,1)S(1)}, u32[]{:S(2)}, u32[]{:S(2)}) async-start(bf16[8,128,1024]{2,1,0:T(8,128)(2,1)} %stack.2), calls=%async_computation | async-start | bytes 4194304 | tf_op jit(solution)/shard_map/all_to_all | solution.py:13
  27.6 0.0 all-gather.5.cloned.1.call-start
  27.7 0.7 all-gather.5.cloned.1.call-update
  28.4 0.0 reduce-scatter.7.cloned.1.call-start
  28.4 56.7 %all-to-all-done = bf16[8,128,1024]{2,1,0:T(8,128)(2,1)S(1)} async-done(((bf16[8,128,1024]{2,1,0:T(8,128)(2,1)}), bf16[8,128,1024]{2,1,0:T(8,128)(2,1)S(1)}, u32[]{:S(2)}, u32[]{:S(2)}) %all-to-all-start) | async-done | bytes 2097184 | tf_op jit(solution)/shard_map/all_to_all | solution.py:13
  85.1 0.0 copy-start.1
  85.1 0.0 copy-done.3
  85.1 0.8 convolution_convert_fusion.4
  85.9 0.5 copy-done.1
  86.4 0.0 copy-done
  86.4 0.8 convolution_convert_fusion.5
  87.2 0.0 copy-start.5
  87.2 0.1 pad_maximum_fusion
  87.3 1.3 copy.16
  88.6 0.0 reduce-scatter.7.cloned.1.call-update
  88.6 0.0 all-gather.3.cloned.1.call-start
  88.7 0.0 copy-done.5
  88.7 80.3 %all_gather.12 = bf16[448,1024]{1,0:T(8,128)(2,1)} all-gather(bf16[224,1024]{1,0:T(8,128)(2,1)S(1)} %copy-done.5), channel_id=1, replica_groups=mesh['gx_0'=4,'gx_1'=2,'gy'=8,'gz'=8] {'gx_1'}, dimensions={0}, use_global_device_ids=true | all-gather | bytes 1376256 | tf_op jit(solution)/shard_map/all_gather | solution.py:47
  169.0 0.0 all-gather.3.cloned.1.call-update
  169.0 17.6 %all-gather.5.cloned.1.call-done = bf16[1024,1024]{1,0:T(8,128)(2,1)} async-done(((bf16[128,1024]{1,0:T(8,128)(2,1)}), bf16[1024,1024]{1,0:T(8,128)(2,1)}) %all-gather.5.cloned.1.call-update) | async-done | bytes 2097168 | tf_op jit(solution)/shard_map/all_gather | solution.py:119
  186.6 2.4 fusion
  189.0 0.1 copy.27
  189.1 12.8 %all_to_all.41 = bf16[8,128,224]{1,2,0:T(8,128)(2,1)S(1)} all-to-all(bf16[8,128,224]{1,2,0:T(8,128)(2,1)S(1)} %bitcast.39), channel_id=1, replica_groups=mesh['gx_0'=4,'gx_1'=2,'gy'=8,'gz'=8] {'gz'}, dimensions={0} | all-to-all | bytes 917504 | tf_op jit(solution)/shard_map/all_to_all | solution.py:63
  201.8 0.1 convert_reduce_fusion
  201.9 67.1 %reduce-scatter.7.cloned.1.call-done = bf16[128,448]{1,0:T(8,128)(2,1)} async-done(((bf16[1024,448]{1,0:T(8,128)(2,1)}), bf16[128,448]{1,0:T(8,128)(2,1)}) %reduce-scatter.7.cloned.1.call-update) | async-done | bytes 114704
  269.0 1.1 fusion.20
  270.0 0.1 copy.18
  270.1 0.1 copy.19
  270.3 0.1 fusion.13
  270.4 0.1 broadcast_in_dim.6
  270.4 14.8 %all_to_all.42 = bf16[8,128,224]{1,2,0:T(8,128)(2,1)} all-to-all(bf16[8,128,224]{1,2,0:T(8,128)(2,1)S(1)} %broadcast_in_dim.6), channel_id=1, replica_groups=mesh['gx_0'=4,'gx_1'=2,'gy'=8,'gz'=8] {'gz'}, dimensions={0} | all-to-all | bytes 917504 | tf_op jit(solution)/shard_map/all_to_all | solution.py:28
  285.3 14.6 %all-to-all-start.2 = ((bf16[8,128,224]{1,2,0:T(8,128)(2,1)}), bf16[8,128,224]{1,2,0:T(8,128)(2,1)S(1)}, u32[]{:S(2)}, u32[]{:S(2)}) async-start(bf16[8,128,224]{1,2,0:T(8,128)(2,1)} %all_to_all.42), calls=%async_computation.2 | async-start | bytes 917504 | tf_op jit(solution)/shard_map/all_to_all | solution.py:112
  299.9 29.6 %all-gather.3.cloned.1.call-done = bf16[1792,1024]{1,0:T(8,128)(2,1)} async-done(((bf16[448,1024]{1,0:T(8,128)(2,1)}), bf16[1792,1024]{1,0:T(8,128)(2,1)}) %all-gather.3.cloned.1.call-update) | async-done | bytes 3670032 | tf_op jit(solution)/shard_map/all_gather | solution.py:47
  329.5 0.0 all-to-all-done.2
  329.5 2.7 convolution_convert_fusion.6
  332.2 1.6 broadcast_in_dim.7
  333.9 10.0 %all-to-all-start.3 = ((bf16[8,128,1024]{2,1,0:T(8,128)(2,1)}), bf16[8,128,1024]{2,1,0:T(8,128)(2,1)S(1)}, u32[]{:S(2)}, u32[]{:S(2)}) async-start(bf16[8,128,1024]{2,1,0:T(8,128)(2,1)} %broadcast_in_dim.7), calls=%async_computation.3 | async-start | bytes 4194304 | tf_op jit(solution)/shard_map/all_to_all | solution.py:28
  343.9 0.0 reduce-scatter.5.cloned.1.call-start
  343.9 14.3 %all_gather.15 = bf16[1024,448]{0,1:T(8,128)(2,1)S(1)} all-gather(bf16[128,448]{0,1:T(8,128)(2,1)S(1)} %pad_maximum_fusion.1), channel_id=1, replica_groups=mesh['gx_0'=4,'gx_1'=2,'gy'=8,'gz'=8] {'gz'}, dimensions={0}, use_global_device_ids=true | all-gather | bytes 1032192 | tf_op jit(solution)/shard_map/all_gather | solution.py:70
  358.2 0.0 copy-start.4
  358.2 0.7 fusion.8
  358.9 0.3 copy-done.4
  359.2 2.1 add_convert_fusion
  361.3 0.0 reduce-scatter.5.cloned.1.call-update
  361.4 184.4 %reduce-scatter.5.cloned.1.call-done = bf16[128,1024]{1,0:T(8,128)(2,1)} async-done(((bf16[1024,1024]{1,0:T(8,128)(2,1)}), bf16[128,1024]{1,0:T(8,128)(2,1)}) %reduce-scatter.5.cloned.1.call-update) | async-done | bytes 262160 | tf_op jit(solution)/shard_map/reduce_scatter | solution.py:124
  545.8 0.0 all-to-all-done.3
  545.8 2.6 broadcast_in_dim.8
  548.4 4.3 all-to-all-start.5
  552.8 0.0 copy-start.2
  552.8 3.2 fusion.1
  555.9 0.0 copy-done.2
  555.9 0.0 copy-start.6
  555.9 1.4 fusion.2
  557.3 0.2 copy-done.6
  557.5 2.4 convolution_convert_fusion
  560.0 1.1 reduce_sum.33
  561.0 86.6 %all-to-all-done.5 = bf16[8,128,1024]{2,1,0:T(8,128)(2,1)} async-done(((bf16[8,128,1024]{2,1,0:T(8,128)(2,1)}), bf16[8,128,1024]{2,1,0:T(8,128)(2,1)}, u32[]{:S(2)}, u32[]{:S(2)}) %all-to-all-start.5) | async-done | bytes 2097184 | tf_op jit(solution)/shard_map/all_to_all | solution.py:28
  647.6 2.7 reduce_sum.35
  (1 shorter events, 0.0 us)
Async XLA Ops:
  7.2 79.3 %copy-start = (bf16[1024,224]{0,1:T(8,128)(2,1)S(1)}, bf16[1024,224]{0,1:T(8,128)(2,1)}, u32[]{:S(2)}) copy-start(bf16[1024,224]{0,1:T(8,128)(2,1)} %param.6) | copy-start | bytes 1376260
  9.8 75.3 %copy-start.3 = (bf16[1024,224]{0,1:T(8,128)(2,1)S(1)}, bf16[1024,224]{0,1:T(8,128)(2,1)}, u32[]{:S(2)}) copy-start(bf16[1024,224]{0,1:T(8,128)(2,1)} %param.7) | copy-start | bytes 1376260
  9.8 75.3 %all-to-all-start = ((bf16[8,128,1024]{2,1,0:T(8,128)(2,1)}), bf16[8,128,1024]{2,1,0:T(8,128)(2,1)S(1)}, u32[]{:S(2)}, u32[]{:S(2)}) async-start(bf16[8,128,1024]{2,1,0:T(8,128)(2,1)} %stack.2), calls=%async_computation | async-start | bytes 4194304 | tf_op jit(solution)/shard_map/all_to_all | solution.py:13
  27.6 158.9 %all-gather.5.cloned.1.call-start = ((), (), s32[]{:S(2)}) async-start(), calls=%async_computation.9 | async-start | bytes 2359296 | tf_op jit(solution)/shard_map/all_gather | solution.py:119
  28.4 240.6 %reduce-scatter.7.cloned.1.call-start = ((), (), s32[]{:S(2)}) async-start(), calls=%async_computation.11 | async-start | bytes 1179648
  85.1 1.3 copy-start.1
  87.2 1.4 copy-start.5
  88.6 240.9 %all-gather.3.cloned.1.call-start = ((), (), s32[]{:S(2)}) async-start(), calls=%async_computation.8 | async-start | bytes 4587520 | tf_op jit(solution)/shard_map/all_gather | solution.py:47
  285.3 44.3 %all-to-all-start.2 = ((bf16[8,128,224]{1,2,0:T(8,128)(2,1)}), bf16[8,128,224]{1,2,0:T(8,128)(2,1)S(1)}, u32[]{:S(2)}, u32[]{:S(2)}) async-start(bf16[8,128,224]{1,2,0:T(8,128)(2,1)} %all_to_all.42), calls=%async_computation.2 | async-start | bytes 917504 | tf_op jit(solution)/shard_map/all_to_all | solution.py:112
  333.9 211.9 %all-to-all-start.3 = ((bf16[8,128,1024]{2,1,0:T(8,128)(2,1)}), bf16[8,128,1024]{2,1,0:T(8,128)(2,1)S(1)}, u32[]{:S(2)}, u32[]{:S(2)}) async-start(bf16[8,128,1024]{2,1,0:T(8,128)(2,1)} %broadcast_in_dim.7), calls=%async_computation.3 | async-start | bytes 4194304 | tf_op jit(solution)/shard_map/all_to_all | solution.py:28
  343.9 202.0 %reduce-scatter.5.cloned.1.call-start = ((), (), s32[]{:S(2)}) async-start(), calls=%async_computation.10 | async-start | bytes 2359296 | tf_op jit(solution)/shard_map/reduce_scatter | solution.py:124
  358.2 1.0 copy-start.4
  548.4 99.2 %all-to-all-start.5 = ((bf16[8,128,1024]{2,1,0:T(8,128)(2,1)}), bf16[8,128,1024]{2,1,0:T(8,128)(2,1)}, u32[]{:S(2)}, u32[]{:S(2)}) async-start(bf16[8,128,1024]{2,1,0:T(8,128)(2,1)} %broadcast_in_dim.8), calls=%async_computation.6 | async-start | bytes 4194304 | tf_op jit(solution)/shard_map/all_to_all | solution.py:28
  552.8 3.2 copy-start.2
  555.9 1.6 copy-start.6
Sparse Core Ops, SparseCore 0:
  31.6 154.8 all-gather.4
  189.4 79.5 reduce-scatter.6
  271.1 58.3 all-gather.2
  361.5 184.2 reduce-scatter.4
